TPU v7x, 32 devices: a whole 2x2x4 slice. The times are simulated.
32 devices in a mesh: wide: 4 (over z), narrow: 8 (over y, x, core).
Axes of the slice: x: 2, y: 2, z: 4, core: 2. Of those that a mesh axis runs over, the one named last changes fastest.
Arguments:
- sources: bfloat16 [32768, 768], P(('wide', 'narrow')), as said below
- targets: bfloat16 [32768, 768], P(('wide', 'narrow')), as said below
- target_lists: int32 [256, 4], P(('wide', 'narrow')), may hold values from 0 to 255, as said below
- target_clusters: int32 [32768], P(('wide', 'narrow')), may hold values from 0 to 8191
- centroids_src: bfloat16 [8192, 768], P(('wide', 'narrow')), may hold values from -6 to 6
- centroids_tgt: bfloat16 [8192, 768], P('narrow', 'wide'), may hold values from -6 to 6
- sender_mean_measure: float32 [8192], P('wide'), may hold values from 0.05 to 20
- recipient_mean_measure: float32 [8192], P('narrow'), may hold values from 0.05 to 20
Outputs:
- src_bary: bfloat16 [32768, 768], P(('wide', 'narrow'))
- tgt_bary: bfloat16 [32768, 768], P(('wide', 'narrow'))
- src_potential: float32 [32768], P(('wide', 'narrow'))
- tgt_potential: float32 [32768], P(('wide', 'narrow'))
Inputs may be any that keep to these rules, and one draw needn't show every extreme that they name: `target_lists`: target block t holds targets t * 128 to (t + 1) * 128 - 1. Every entry names a block held by a device with the same wide index as the device of the source block. Among the 32 entries of one device, at most 5 name blocks held by any one device, and on every device some device is named by exactly 5. Every target block is named by at least one entry. `sources`: Real-valued features. `targets`: Real-valued features.
All inputs are finite; a program needn't handle non-finite values.
Results may differ from a plain program's by a relative error of at most 0.007.
Values may be sent and summed in bfloat16 or wider, within the bound.
A program may use at most 128 MiB of HBM per device.

v0:
```python
import jax
import jax.numpy as jnp
from jax import lax
from jax.sharding import PartitionSpec as P

BLK = 128
LIST = 4
ITC = 6
STEPS = 3
heat_parameter = 0.02


def contract_rows(left_rows, right_rows):
    return lax.dot_general(
        left_rows, right_rows, (((1,), (1,)), ((), ())), preferred_element_type=jnp.float32
    )


def square_norms(rows_in):
    return jnp.sum(jnp.square(rows_in.astype(jnp.float32)), axis=-1)


def lateral_lse_offset(rating_grid_form):
    best_rating = lax.pmax(jnp.max(rating_grid_form, axis=1), "narrow")
    ongoing_additions = lax.psum(
        jnp.sum(jnp.exp(rating_grid_form - best_rating[:, None]), axis=1), "narrow"
    )
    return best_rating + jnp.log(ongoing_additions)


def vertical_lse_offset(rating_grid_form):
    best_rating = lax.pmax(jnp.max(rating_grid_form, axis=0), "wide")
    ongoing_additions = lax.psum(
        jnp.sum(jnp.exp(rating_grid_form - best_rating[None, :]), axis=0), "wide"
    )
    return best_rating + jnp.log(ongoing_additions)


def body(
    sources,
    targets,
    target_lists,
    target_clusters,
    centroids_src,
    centroids_tgt,
    sender_mean_measure,
    recipient_mean_measure,
):
    feature_count = sources.shape[1]
    narrow_count = lax.axis_size("narrow")
    col_panel = lax.all_gather(centroids_tgt, "wide", axis=1, tiled=True)
    col_sq = square_norms(col_panel)
    fragment = lax.all_gather(centroids_src, "narrow", axis=0, tiled=True)
    blurred_stratum = (
        square_norms(fragment)[:, None] + col_sq[None, :] - 2.0 * contract_rows(fragment, col_panel)
    ) / feature_count
    ln_sender_measure = heat_parameter * jnp.log(sender_mean_measure)
    ln_recipient_measure = heat_parameter * jnp.log(recipient_mean_measure)

    def coarse_turn(iteration, recipient_blurred_stratum):
        sender_blurred_stratum = ln_sender_measure - heat_parameter * lateral_lse_offset(
            (recipient_blurred_stratum[None, :] - blurred_stratum) / heat_parameter
        )
        return ln_recipient_measure - heat_parameter * vertical_lse_offset(
            (sender_blurred_stratum[:, None] - blurred_stratum) / heat_parameter
        )

    coarse_cols = lax.fori_loop(
        0, ITC, coarse_turn, jnp.zeros((blurred_stratum.shape[1],), jnp.float32)
    )
    coarse_all = lax.all_gather(coarse_cols, "narrow", axis=0, tiled=True)
    src_blocks = sources.reshape(-1, BLK, feature_count)
    tgt_blocks = targets.reshape(-1, BLK, feature_count)
    src_count = src_blocks.shape[0]
    tgt_count = tgt_blocks.shape[0]
    capacity = max(
        (5 * src_count * LIST + 4 * narrow_count - 1) // (4 * narrow_count),
        (tgt_count + narrow_count - 1) // narrow_count,
    )
    slot_count = narrow_count * capacity
    wanted = target_lists.reshape(-1)
    entries = wanted.shape[0]
    entry_index = jnp.arange(entries, dtype=jnp.int32)
    owner_of = wanted // tgt_count % narrow_count
    local_block = wanted % tgt_count
    earlier = jnp.logical_and(
        owner_of[:, None] == owner_of[None, :], entry_index[None, :] < entry_index[:, None]
    )
    rank_of = jnp.sum(earlier.astype(jnp.int32), axis=1)
    slot_of = owner_of * capacity + rank_of
    requests = (
        jnp.full((slot_count,), -1, jnp.int32)
        .at[slot_of]
        .set(local_block)
        .reshape(narrow_count, capacity)
    )

    def into_slots(values):
        return jnp.zeros((slot_count,) + values.shape[1:], values.dtype).at[slot_of].set(values)

    asked_ids = lax.all_to_all(requests, "narrow", split_axis=0, concat_axis=0, tiled=True)
    found = jnp.take(tgt_blocks, jnp.clip(asked_ids, 0, tgt_count - 1), axis=0)
    received, asked_ids = (
        lax.all_to_all(
            jnp.where((asked_ids >= 0)[:, :, None, None], found, jnp.zeros((), jnp.bfloat16)),
            "narrow",
            split_axis=0,
            concat_axis=0,
            tiled=True,
        ),
        asked_ids,
    )
    rows_entry = jnp.take(
        received.reshape(slot_count, BLK, feature_count), slot_of, axis=0
    ).reshape(src_count, LIST, BLK, feature_count)
    src_sq = square_norms(src_blocks)
    rows_sq = square_norms(rows_entry)
    cross_term = jnp.einsum(
        "bid,blcd->blic", src_blocks, rows_entry, preferred_element_type=jnp.float32
    )
    pointwise_charge = (
        src_sq[:, None, :, None] + rows_sq[:, :, None, :] - 2.0 * cross_term
    ) / feature_count
    flat_asked = asked_ids.reshape(-1)
    slot_live = flat_asked >= 0
    clipped_asked = jnp.clip(flat_asked, 0, tgt_count - 1)
    slot_pick = flat_asked[None, :] == jnp.arange(tgt_count, dtype=jnp.int32)[:, None]
    recipient_kantorovich = jnp.take(coarse_all, target_clusters, axis=0).reshape(tgt_count, BLK)

    def send_potentials(values):
        outgoing = jnp.where(
            slot_live[:, None], jnp.take(values, clipped_asked, axis=0), 0.0
        ).reshape(narrow_count, capacity, BLK)
        back = lax.all_to_all(outgoing, "narrow", split_axis=0, concat_axis=0, tiled=True)
        return jnp.take(back.reshape(slot_count, BLK), slot_of, axis=0).reshape(
            src_count, LIST, BLK
        )

    sender_kantorovich = jnp.zeros((src_count, BLK), jnp.float32)
    for iteration in range(STEPS):
        named_kantorovich = send_potentials(recipient_kantorovich)
        rating_grid_form = (named_kantorovich[:, :, None, :] - pointwise_charge) / heat_parameter
        best_rating = jnp.max(rating_grid_form, axis=(1, 3))
        sender_kantorovich = -heat_parameter * (
            best_rating
            + jnp.log(
                jnp.sum(jnp.exp(rating_grid_form - best_rating[:, None, :, None]), axis=(1, 3))
            )
        )
        reverse_score_matrix = (
            sender_kantorovich[:, None, :, None] - pointwise_charge
        ) / heat_parameter
        part_top = jnp.max(reverse_score_matrix, axis=2)
        part_sum = jnp.sum(jnp.exp(reverse_score_matrix - part_top[:, :, None, :]), axis=2)
        top_slots = into_slots(part_top.reshape(entries, BLK)).reshape(narrow_count, capacity, BLK)
        sum_slots = into_slots(part_sum.reshape(entries, BLK)).reshape(narrow_count, capacity, BLK)
        top_back, sum_back = (
            lax.all_to_all(top_slots, "narrow", split_axis=0, concat_axis=0, tiled=True),
            lax.all_to_all(sum_slots, "narrow", split_axis=0, concat_axis=0, tiled=True),
        )
        flat_top = top_back.reshape(slot_count, BLK)
        flat_sum = sum_back.reshape(slot_count, BLK)
        largest_figure = jnp.max(
            jnp.where(slot_pick[:, :, None], flat_top[None, :, :], -jnp.inf), axis=1
        )
        ongoing_additions = jnp.sum(
            jnp.where(
                slot_pick[:, :, None],
                flat_sum[None, :, :] * jnp.exp(flat_top[None, :, :] - largest_figure[:, None, :]),
                0.0,
            ),
            axis=1,
        )
        recipient_kantorovich = -heat_parameter * (largest_figure + jnp.log(ongoing_additions))
    named_kantorovich = send_potentials(recipient_kantorovich)
    joint_measure_shares_entrywise = jnp.exp(
        (sender_kantorovich[:, None, :, None] + named_kantorovich[:, :, None, :] - pointwise_charge)
        / heat_parameter
    ).astype(jnp.bfloat16)
    src_num = jnp.einsum(
        "blic,blcd->bid",
        joint_measure_shares_entrywise,
        rows_entry,
        preferred_element_type=jnp.float32,
    )
    src_den = jnp.sum(joint_measure_shares_entrywise, axis=(1, 3), dtype=jnp.float32)
    src_bary = (src_num / src_den[:, :, None]).astype(jnp.bfloat16).reshape(-1, feature_count)
    entry_rows = jnp.einsum(
        "blic,bid->blcd",
        joint_measure_shares_entrywise,
        src_blocks,
        preferred_element_type=jnp.float32,
    ).astype(jnp.bfloat16)
    entry_mass = jnp.sum(joint_measure_shares_entrywise, axis=2, dtype=jnp.float32).astype(
        jnp.bfloat16
    )
    row_slots = into_slots(entry_rows.reshape(entries, BLK, feature_count)).reshape(
        narrow_count, capacity, BLK, feature_count
    )
    mass_slots = into_slots(entry_mass.reshape(entries, BLK)).reshape(narrow_count, capacity, BLK)
    numerator, denominator = (
        lax.all_to_all(row_slots, "narrow", split_axis=0, concat_axis=0, tiled=True),
        lax.all_to_all(mass_slots, "narrow", split_axis=0, concat_axis=0, tiled=True),
    )
    numerator = numerator.reshape(slot_count, BLK, feature_count)
    denominator = denominator.reshape(slot_count, BLK)
    picker = slot_pick.astype(jnp.bfloat16)
    tgt_num = jnp.dot(
        picker,
        numerator.reshape(slot_count, BLK * feature_count),
        preferred_element_type=jnp.float32,
    ).reshape(tgt_count, BLK, feature_count)
    tgt_den = jnp.dot(picker, denominator, preferred_element_type=jnp.float32)
    tgt_bary = (tgt_num / tgt_den[:, :, None]).astype(jnp.bfloat16).reshape(-1, feature_count)
    return (src_bary, tgt_bary, sender_kantorovich.reshape(-1), recipient_kantorovich.reshape(-1))


def solution(mesh):
    in_specs = (
        P(("wide", "narrow"), None),
        P(("wide", "narrow"), None),
        P(("wide", "narrow"), None),
        P(("wide", "narrow")),
        P(("wide", "narrow"), None),
        P("narrow", "wide"),
        P("wide"),
        P("narrow"),
    )
    out_specs = (
        P(("wide", "narrow"), None),
        P(("wide", "narrow"), None),
        P(("wide", "narrow")),
        P(("wide", "narrow")),
    )
    return jax.shard_map(body, mesh=mesh, in_specs=in_specs, out_specs=out_specs, check_vma=False)
```

profile of v0, /device:TPU:0, one launch (start us, length us, event | category | flops | bytes accessed | tf_op | source)
XLA Modules:
  0.0 826.7 jit_solution(1483100814059321418)
XLA Ops:
  11.2 5.2 all-to-all-start
  22.5 5.8 gather_fusion.1
  28.4 20.9 %all-gather.5.cloned.1.call-done = bf16[1024,768]{0,1:T(8,128)(2,1)} async-done(((bf16[1024,192]{0,1:T(8,128)(2,1)}), bf16[1024,768]{0,1:T(8,128)(2,1)}) %all-gather.5.cloned.1.call-update) | async-done | bytes 1572880 | tf_op jit(solution)/shard_map/all_gather | solution.py:51
  51.2 31.1 %all-gather.3.cloned.1.call-done = bf16[2048,768]{1,0:T(8,128)(2,1)} async-done(((bf16[256,768]{1,0:T(8,128)(2,1)}), bf16[2048,768]{1,0:T(8,128)(2,1)}) %all-gather.3.cloned.1.call-update) | async-done | bytes 3145744 | tf_op jit(solution)/shard_map/all_gather | solution.py:53
  85.1 5.7 subtract_multiply_fusion.2
  90.8 362.7 %while.11 = (s32[]{:T(128)}, f32[1024]{0:T(1024)S(1)}, f32[2048,1024]{1,0:T(8,128)}, f32[2048]{0:T(1024)S(1)}, f32[1024]{0:T(1024)S(1)}, /*index=5*/s32[]{:T(128)}, s32[]{:T(128)}) while((s32[]{:T(128)}, f32[1024]{0:T(1024)S(1)}, f32[2048,1024]{1,0:T(8,128)}, f32[2048]{0:T(1024)S(1)}, f32[1024]{0:T(1024)S(1)}, ...), condition=%wide.region_13.14_spmd.clone, body=%wide.region_4.13_spmd.clone.sunk | while | flops 29370372 | bytes 33722456 | solution.py:68
  95.1 13.3 %pmax.18 = f32[2048]{0:T(1024)S(1)} all-reduce(f32[2048]{0:T(1024)S(1)} %fusion.63), channel_id=1, replica_groups=mesh['wide'=4,'narrow'=8] {'narrow'}, use_global_device_ids=true, to_apply=%region_6.0 | all-reduce | flops 2048 | bytes 16384 | tf_op jit(solution)/shard_map/while/body/eval_jaxpr/pmax | solution.py:24
  108.5 4.4 exponential_reduce_fusion.10
  112.9 12.0 %psum.18 = f32[2048]{0:T(1024)S(1)} all-reduce(f32[2048]{0:T(1024)S(1)} %exponential_reduce_fusion.10), channel_id=1, replica_groups=mesh['wide'=4,'narrow'=8] {'narrow'}, use_global_device_ids=true, to_apply=%region_8.0 | all-reduce | flops 2048 | bytes 16384 | tf_op jit(solution)/shard_map/while/body/eval_jaxpr/psum | solution.py:25
  128.9 11.7 %pmax.19 = f32[1024]{0:T(1024)S(1)} all-reduce(f32[1024]{0:T(1024)S(1)} %fusion.64), channel_id=1, replica_groups=mesh['wide'=4,'narrow'=8] {'wide'}, use_global_device_ids=true, to_apply=%region_10.0 | all-reduce | flops 1024 | bytes 8192 | tf_op jit(solution)/shard_map/while/body/eval_jaxpr/pmax | solution.py:32
  140.6 4.4 exponential_reduce_fusion.11
  145.0 8.4 %psum.19 = f32[1024]{0:T(1024)S(1)} all-reduce(f32[1024]{0:T(1024)S(1)} %exponential_reduce_fusion.11), channel_id=1, replica_groups=mesh['wide'=4,'narrow'=8] {'wide'}, use_global_device_ids=true, to_apply=%region_12.12 | all-reduce | flops 1024 | bytes 8192 | tf_op jit(solution)/shard_map/while/body/eval_jaxpr/psum | solution.py:33
  153.4 4.3 fusion.63
  157.7 12.0 %pmax.18 = f32[2048]{0:T(1024)S(1)} all-reduce(f32[2048]{0:T(1024)S(1)} %fusion.63), channel_id=1, replica_groups=mesh['wide'=4,'narrow'=8] {'narrow'}, use_global_device_ids=true, to_apply=%region_6.0 | all-reduce | flops 2048 | bytes 16384 | tf_op jit(solution)/shard_map/while/body/eval_jaxpr/pmax | solution.py:24
  169.8 4.4 exponential_reduce_fusion.10
  174.2 12.0 %psum.18 = f32[2048]{0:T(1024)S(1)} all-reduce(f32[2048]{0:T(1024)S(1)} %exponential_reduce_fusion.10), channel_id=1, replica_groups=mesh['wide'=4,'narrow'=8] {'narrow'}, use_global_device_ids=true, to_apply=%region_8.0 | all-reduce | flops 2048 | bytes 16384 | tf_op jit(solution)/shard_map/while/body/eval_jaxpr/psum | solution.py:25
  190.2 10.4 %pmax.19 = f32[1024]{0:T(1024)S(1)} all-reduce(f32[1024]{0:T(1024)S(1)} %fusion.64), channel_id=1, replica_groups=mesh['wide'=4,'narrow'=8] {'wide'}, use_global_device_ids=true, to_apply=%region_10.0 | all-reduce | flops 1024 | bytes 8192 | tf_op jit(solution)/shard_map/while/body/eval_jaxpr/pmax | solution.py:32
  200.6 4.4 exponential_reduce_fusion.11
  205.0 8.4 %psum.19 = f32[1024]{0:T(1024)S(1)} all-reduce(f32[1024]{0:T(1024)S(1)} %exponential_reduce_fusion.11), channel_id=1, replica_groups=mesh['wide'=4,'narrow'=8] {'wide'}, use_global_device_ids=true, to_apply=%region_12.12 | all-reduce | flops 1024 | bytes 8192 | tf_op jit(solution)/shard_map/while/body/eval_jaxpr/psum | solution.py:33
  213.4 4.3 fusion.63
  217.7 12.0 %pmax.18 = f32[2048]{0:T(1024)S(1)} all-reduce(f32[2048]{0:T(1024)S(1)} %fusion.63), channel_id=1, replica_groups=mesh['wide'=4,'narrow'=8] {'narrow'}, use_global_device_ids=true, to_apply=%region_6.0 | all-reduce | flops 2048 | bytes 16384 | tf_op jit(solution)/shard_map/while/body/eval_jaxpr/pmax | solution.py:24
  229.7 4.4 exponential_reduce_fusion.10
  234.2 12.0 %psum.18 = f32[2048]{0:T(1024)S(1)} all-reduce(f32[2048]{0:T(1024)S(1)} %exponential_reduce_fusion.10), channel_id=1, replica_groups=mesh['wide'=4,'narrow'=8] {'narrow'}, use_global_device_ids=true, to_apply=%region_8.0 | all-reduce | flops 2048 | bytes 16384 | tf_op jit(solution)/shard_map/while/body/eval_jaxpr/psum | solution.py:25
  250.2 10.4 %pmax.19 = f32[1024]{0:T(1024)S(1)} all-reduce(f32[1024]{0:T(1024)S(1)} %fusion.64), channel_id=1, replica_groups=mesh['wide'=4,'narrow'=8] {'wide'}, use_global_device_ids=true, to_apply=%region_10.0 | all-reduce | flops 1024 | bytes 8192 | tf_op jit(solution)/shard_map/while/body/eval_jaxpr/pmax | solution.py:32
  260.6 4.4 exponential_reduce_fusion.11
  265.0 8.4 %psum.19 = f32[1024]{0:T(1024)S(1)} all-reduce(f32[1024]{0:T(1024)S(1)} %exponential_reduce_fusion.11), channel_id=1, replica_groups=mesh['wide'=4,'narrow'=8] {'wide'}, use_global_device_ids=true, to_apply=%region_12.12 | all-reduce | flops 1024 | bytes 8192 | tf_op jit(solution)/shard_map/while/body/eval_jaxpr/psum | solution.py:33
  277.7 12.0 %pmax.18 = f32[2048]{0:T(1024)S(1)} all-reduce(f32[2048]{0:T(1024)S(1)} %fusion.63), channel_id=1, replica_groups=mesh['wide'=4,'narrow'=8] {'narrow'}, use_global_device_ids=true, to_apply=%region_6.0 | all-reduce | flops 2048 | bytes 16384 | tf_op jit(solution)/shard_map/while/body/eval_jaxpr/pmax | solution.py:24
  289.7 4.4 exponential_reduce_fusion.10
  294.2 12.0 %psum.18 = f32[2048]{0:T(1024)S(1)} all-reduce(f32[2048]{0:T(1024)S(1)} %exponential_reduce_fusion.10), channel_id=1, replica_groups=mesh['wide'=4,'narrow'=8] {'narrow'}, use_global_device_ids=true, to_apply=%region_8.0 | all-reduce | flops 2048 | bytes 16384 | tf_op jit(solution)/shard_map/while/body/eval_jaxpr/psum | solution.py:25
  310.2 10.4 %pmax.19 = f32[1024]{0:T(1024)S(1)} all-reduce(f32[1024]{0:T(1024)S(1)} %fusion.64), channel_id=1, replica_groups=mesh['wide'=4,'narrow'=8] {'wide'}, use_global_device_ids=true, to_apply=%region_10.0 | all-reduce | flops 1024 | bytes 8192 | tf_op jit(solution)/shard_map/while/body/eval_jaxpr/pmax | solution.py:32
  320.6 4.4 exponential_reduce_fusion.11
  325.0 8.4 %psum.19 = f32[1024]{0:T(1024)S(1)} all-reduce(f32[1024]{0:T(1024)S(1)} %exponential_reduce_fusion.11), channel_id=1, replica_groups=mesh['wide'=4,'narrow'=8] {'wide'}, use_global_device_ids=true, to_apply=%region_12.12 | all-reduce | flops 1024 | bytes 8192 | tf_op jit(solution)/shard_map/while/body/eval_jaxpr/psum | solution.py:33
  337.7 12.1 %pmax.18 = f32[2048]{0:T(1024)S(1)} all-reduce(f32[2048]{0:T(1024)S(1)} %fusion.63), channel_id=1, replica_groups=mesh['wide'=4,'narrow'=8] {'narrow'}, use_global_device_ids=true, to_apply=%region_6.0 | all-reduce | flops 2048 | bytes 16384 | tf_op jit(solution)/shard_map/while/body/eval_jaxpr/pmax | solution.py:24
  349.7 4.4 exponential_reduce_fusion.10
  354.2 12.1 %psum.18 = f32[2048]{0:T(1024)S(1)} all-reduce(f32[2048]{0:T(1024)S(1)} %exponential_reduce_fusion.10), channel_id=1, replica_groups=mesh['wide'=4,'narrow'=8] {'narrow'}, use_global_device_ids=true, to_apply=%region_8.0 | all-reduce | flops 2048 | bytes 16384 | tf_op jit(solution)/shard_map/while/body/eval_jaxpr/psum | solution.py:25
  370.3 10.4 %pmax.19 = f32[1024]{0:T(1024)S(1)} all-reduce(f32[1024]{0:T(1024)S(1)} %fusion.64), channel_id=1, replica_groups=mesh['wide'=4,'narrow'=8] {'wide'}, use_global_device_ids=true, to_apply=%region_10.0 | all-reduce | flops 1024 | bytes 8192 | tf_op jit(solution)/shard_map/while/body/eval_jaxpr/pmax | solution.py:32
  380.7 4.4 exponential_reduce_fusion.11
  385.1 8.4 %psum.19 = f32[1024]{0:T(1024)S(1)} all-reduce(f32[1024]{0:T(1024)S(1)} %exponential_reduce_fusion.11), channel_id=1, replica_groups=mesh['wide'=4,'narrow'=8] {'wide'}, use_global_device_ids=true, to_apply=%region_12.12 | all-reduce | flops 1024 | bytes 8192 | tf_op jit(solution)/shard_map/while/body/eval_jaxpr/psum | solution.py:33
  393.5 4.3 fusion.63
  397.7 12.1 %pmax.18 = f32[2048]{0:T(1024)S(1)} all-reduce(f32[2048]{0:T(1024)S(1)} %fusion.63), channel_id=1, replica_groups=mesh['wide'=4,'narrow'=8] {'narrow'}, use_global_device_ids=true, to_apply=%region_6.0 | all-reduce | flops 2048 | bytes 16384 | tf_op jit(solution)/shard_map/while/body/eval_jaxpr/pmax | solution.py:24
  409.9 4.4 exponential_reduce_fusion.10
  414.3 12.1 %psum.18 = f32[2048]{0:T(1024)S(1)} all-reduce(f32[2048]{0:T(1024)S(1)} %exponential_reduce_fusion.10), channel_id=1, replica_groups=mesh['wide'=4,'narrow'=8] {'narrow'}, use_global_device_ids=true, to_apply=%region_8.0 | all-reduce | flops 2048 | bytes 16384 | tf_op jit(solution)/shard_map/while/body/eval_jaxpr/psum | solution.py:25
  430.4 10.4 %pmax.19 = f32[1024]{0:T(1024)S(1)} all-reduce(f32[1024]{0:T(1024)S(1)} %fusion.64), channel_id=1, replica_groups=mesh['wide'=4,'narrow'=8] {'wide'}, use_global_device_ids=true, to_apply=%region_10.0 | all-reduce | flops 1024 | bytes 8192 | tf_op jit(solution)/shard_map/while/body/eval_jaxpr/pmax | solution.py:32
  440.8 4.4 exponential_reduce_fusion.11
  445.2 8.4 %psum.19 = f32[1024]{0:T(1024)S(1)} all-reduce(f32[1024]{0:T(1024)S(1)} %exponential_reduce_fusion.11), channel_id=1, replica_groups=mesh['wide'=4,'narrow'=8] {'wide'}, use_global_device_ids=true, to_apply=%region_12.12 | all-reduce | flops 1024 | bytes 8192 | tf_op jit(solution)/shard_map/while/body/eval_jaxpr/psum | solution.py:33
  453.6 9.9 %all_gather.11 = f32[8192]{0:T(1024)S(1)} all-gather(f32[1024]{0:T(1024)S(1)} %get-tuple-element.33), channel_id=1, replica_groups=mesh['wide'=4,'narrow'=8] {'narrow'}, dimensions={0}, use_global_device_ids=true | all-gather | bytes 36864 | tf_op jit(solution)/shard_map/all_gather | solution.py:71
  463.4 6.1 gather_fusion
  474.3 7.3 select_select_fusion
  481.5 5.2 all-to-all-start.2
  488.0 87.1 %all-to-all-done.2 = bf16[8,5,128,768]{3,2,1,0:T(8,128)(2,1)} async-done(((bf16[8,5,128,768]{3,2,1,0:T(8,128)(2,1)}), bf16[8,5,128,768]{3,2,1,0:T(8,128)(2,1)}, u32[]{:S(2)}, u32[]{:S(2)}) %all-to-all-start.2) | async-done | bytes 7864352 | tf_op jit(solution)/shard_map/all_to_all | solution.py:104
  575.1 6.8 gather_fusion.2
  581.9 4.7 multiply_reduce_fusion
  604.5 4.6 all-to-all-done.4
  609.9 7.2 all_to_all.74
  635.4 4.6 all-to-all-done.7
  640.8 7.2 all_to_all.75
  666.3 4.6 all-to-all-done.10
  671.8 7.2 all_to_all.76
  686.9 4.4 convolution_convert_fusion
  695.3 20.0 %scatter_fusion = bf16[40,128,768]{2,1,0:T(8,128)(2,1)} fusion(bf16[40,128,768]{2,1,0:T(8,128)(2,1)} %broadcast_in_dim.228, s32[32]{0:T(128)S(1)} %fusion.48, bf16[32,128,768]{2,1,0:T(8,128)(2,1)} %bitcast.96), kind=kCustom, calls=%fused_computation.18 | custom fusion | bytes 18874496 | tf_op jit(solution)/shard_map/scatter | solution.py:99
  715.3 4.9 all-to-all-start.12
  720.4 5.2 fusion.7
  725.8 82.9 %all-to-all-done.12 = bf16[8,5,128,768]{3,2,1,0:T(8,128)(2,1)} async-done(((bf16[8,5,128,768]{3,2,1,0:T(8,128)(2,1)}), bf16[8,5,128,768]{3,2,1,0:T(8,128)(2,1)}, u32[]{:S(2)}, u32[]{:S(2)}) %all-to-all-start.12) | async-done | bytes 7864352 | tf_op jit(solution)/shard_map/all_to_all | solution.py:202
  808.7 9.7 %divide_convert_fusion = bf16[8,128,768]{2,0,1:T(8,128)(2,1)S(1)} fusion(f32[8,128]{0,1:T(8,128)S(1)} %fusion.41, s32[40]{0:T(128)S(1)} %reshape.452, bf16[5,8,128,768]{3,2,1,0:T(8,128)(2,1)} %bitcast.46), kind=kOutput, calls=%fused_computation.42 | convolution fusion | flops 64487744 | bytes 9441440 | tf_op jit(solution)/shard_map/dot_general | solution.py:208
  (178 shorter events, 127.5 us)
Async XLA Ops:
  7.2 15.4 %copy-start = (bf16[1024,768]{1,0:T(8,128)(2,1)S(1)}, bf16[1024,768]{1,0:T(8,128)(2,1)}, u32[]{:S(2)}) copy-start(bf16[1024,768]{1,0:T(8,128)(2,1)} %param.15) | copy-start | bytes 4718596
  7.2 42.2 %all-gather.5.cloned.1.call-start = ((), (), s32[]{:S(2)}) async-start(), calls=%async_computation.15 | async-start | bytes 1966080 | tf_op jit(solution)/shard_map/all_gather | solution.py:51
  7.9 74.4 %all-gather.3.cloned.1.call-start = ((), (), s32[]{:S(2)}) async-start(), calls=%async_computation.14 | async-start | bytes 3538944 | tf_op jit(solution)/shard_map/all_gather | solution.py:53
  11.2 9.8 %all-to-all-start = ((s32[8,1,5]{2,1,0:T(1,128)}), s32[8,1,5]{2,1,0:T(1,128)S(1)}, u32[]{:S(2)}, u32[]{:S(2)}) async-start(s32[8,1,5]{2,1,0:T(1,128)} %bitcast.2), calls=%async_computation | async-start | bytes 8192 | tf_op jit(solution)/shard_map/all_to_all | solution.py:101
  49.3 35.7 %copy-start.9 = (bf16[1024,768]{0,1:T(8,128)(2,1)S(1)}, bf16[1024,768]{0,1:T(8,128)(2,1)}, u32[]{:S(2)}) copy-start(bf16[1024,768]{0,1:T(8,128)(2,1)} %all-gather.5.cloned.1.call-done) | copy-start | bytes 4718596
  82.3 2.8 copy-start.8
  463.4 6.2 copy-start.11
  470.9 10.6 %all-to-all-start.1 = ((f32[8,5,128]{2,1,0:T(8,128)}), f32[8,5,128]{2,1,0:T(8,128)S(1)}, u32[]{:S(2)}, u32[]{:S(2)}) async-start(f32[8,5,128]{2,1,0:T(8,128)} %reshape.453), calls=%async_computation.1 | async-start | bytes 65536 | tf_op jit(solution)/shard_map/all_to_all | solution.py:134
  481.5 5.4 copy-start.7
  481.5 93.6 %all-to-all-start.2 = ((bf16[8,5,128,768]{3,2,1,0:T(8,128)(2,1)}), bf16[8,5,128,768]{3,2,1,0:T(8,128)(2,1)}, u32[]{:S(2)}, u32[]{:S(2)}) async-start(bf16[8,5,128,768]{3,2,1,0:T(8,128)(2,1)} %select_select_fusion), calls=%async_computation.2 | async-start | bytes 15728640 | tf_op jit(solution)/shard_map/all_to_all | solution.py:104
  581.9 4.7 copy-start.5
  590.1 1.4 copy-start.2
  592.8 8.1 all-to-all-start.3
  601.0 8.1 all-to-all-start.4
  617.8 4.1 copy-start.3
  623.8 8.1 all-to-all-start.6
  631.9 8.1 all-to-all-start.7
  648.7 4.1 copy-start.4
  652.8 26.9 %copy-start.10 = (f32[8,128]{1,0:T(8,128)}, f32[8,128]{1,0:T(8,128)S(1)}, u32[]{:S(2)}) copy-start(f32[8,128]{1,0:T(8,128)S(1)} %add_multiply_fusion.1) | copy-start | bytes 12292
  654.7 8.1 all-to-all-start.9
  662.9 8.1 all-to-all-start.10
  671.1 20.1 %copy-start.6 = (f32[8,128]{1,0:T(8,128)}, f32[8,128]{1,0:T(8,128)S(1)}, u32[]{:S(2)}) copy-start(f32[8,128]{1,0:T(8,128)S(1)} %add_multiply_fusion) | copy-start | bytes 12292
  683.5 31.8 %all-to-all-start.13 = ((bf16[8,5,128]{2,1,0:T(8,128)(2,1)}), bf16[8,5,128]{2,1,0:T(8,128)(2,1)S(1)}, u32[]{:S(2)}, u32[]{:S(2)}) async-start(bf16[8,5,128]{2,1,0:T(8,128)(2,1)} %reshape.480), calls=%async_computation.13 | async-start | bytes 32768 | tf_op jit(solution)/shard_map/all_to_all | solution.py:203
  715.3 93.4 %all-to-all-start.12 = ((bf16[8,5,128,768]{3,2,1,0:T(8,128)(2,1)}), bf16[8,5,128,768]{3,2,1,0:T(8,128)(2,1)}, u32[]{:S(2)}, u32[]{:S(2)}) async-start(bf16[8,5,128,768]{3,2,1,0:T(8,128)(2,1)} %bitcast.92), calls=%async_computation.12 | async-start | bytes 15728640 | tf_op jit(solution)/shard_map/all_to_all | solution.py:202
  808.7 11.2 %copy-start.1 = (bf16[1024,768]{1,0:T(8,128)(2,1)S(1)}, bf16[1024,768]{1,0:T(8,128)(2,1)}, u32[]{:S(2)}) copy-start(bf16[1024,768]{1,0:T(8,128)(2,1)} %param.15) | copy-start | bytes 4718596
Sparse Core Ops, SparseCore 0:
  9.6 39.7 all-gather.4
  51.2 31.0 all-gather.2
where the time goes:
time: 829 us; the launch traced here: 827 us
  blocking collectives  292 us (35%)
  waiting for transfers between devices  243 us (29%)
  other arithmetic  145 us (17%)
  local copies, waits for them, and re-layouts  62 us (7%)
  starting transfers between devices  42.1 us (5%)
  matrix products  28.6 us (3%)
  between operations  14.6 us (2%)
    all_to_all x1, waiting for transfers between devices, body(): lax.all_to_all(jnp.where((asked_ids >= 0)[:, :, None, None], found, jnp.z...  87.1 us
    all_to_all x1, waiting for transfers between devices, body(): lax.all_to_all(row_slots, 'narrow', split_axis=0, concat_axis=0, tiled=True)  82.9 us
    pmax x6, blocking collectives, lateral_lse_offset(): best_rating = lax.pmax(jnp.max(rating_grid_form, axis=1), 'narrow')  73.7 us
    psum x6, blocking collectives, lateral_lse_offset(): lax.psum(jnp.sum(jnp.exp(rating_grid_form - best_rating[:, None]), axis=1...  72.4 us
    pmax x6, blocking collectives, vertical_lse_offset(): best_rating = lax.pmax(jnp.max(rating_grid_form, axis=0), 'wide')  63.6 us
    psum x6, blocking collectives, vertical_lse_offset(): lax.psum(jnp.sum(jnp.exp(rating_grid_form - best_rating[None, :]), axis=0...  50.3 us
    all_gather x1, waiting for transfers between devices, body(): fragment = lax.all_gather(centroids_src, 'narrow', axis=0, tiled=True)  31.1 us
    reduce_sum x6, other arithmetic, lateral_lse_offset(): jnp.sum(jnp.exp(rating_grid_form - best_rating[:, None]), axis=1)  26.6 us
  transfers between devices with their start and end apart: 13, of which 11 were waited for; matrix products, arithmetic and copies ran while one was open for 8% of the time, Pallas kernels for 0%

commit v1 on v0

--- a/solution.py
+++ b/solution.py
@@ -2,6 +2,7 @@
 import jax.numpy as jnp
 from jax import lax
 from jax.sharding import PartitionSpec as P
+from jax.lax import axis_index, ppermute, psum
 
 BLK = 128
 LIST = 4
@@ -46,6 +47,25 @@
     sender_mean_measure,
     recipient_mean_measure,
 ):
+
+    def lane_wait(field):
+        side_arr = psum(1, axis_name="narrow")
+        outer = axis_index("narrow")
+        odd, vec_out = (side_arr, outer)
+        big = field.shape[0] // odd
+        newest = jnp.roll(field, -vec_out * big, 0)
+        then = lax.slice_in_dim(newest, 0, big, axis=0)
+        leaves = [then]
+        for at in [*range(1, odd)]:
+            mat_out = lax.slice_in_dim(newest, at * big, (at + 1) * big, axis=0)
+            w_next = ppermute(
+                mat_out, axis_name="narrow", perm=[(tick, (tick + at) % odd) for tick in range(odd)]
+            )
+            leaves.append(w_next)
+        clean = jnp.concatenate(leaves[::-1], 0)
+        block_next = jnp.roll(clean, (vec_out + 1) * leaves[0].shape[0], 0)
+        return block_next
+
     feature_count = sources.shape[1]
     narrow_count = lax.axis_size("narrow")
     col_panel = lax.all_gather(centroids_tgt, "wide", axis=1, tiled=True)
@@ -101,12 +121,8 @@
     asked_ids = lax.all_to_all(requests, "narrow", split_axis=0, concat_axis=0, tiled=True)
     found = jnp.take(tgt_blocks, jnp.clip(asked_ids, 0, tgt_count - 1), axis=0)
     received, asked_ids = (
-        lax.all_to_all(
-            jnp.where((asked_ids >= 0)[:, :, None, None], found, jnp.zeros((), jnp.bfloat16)),
-            "narrow",
-            split_axis=0,
-            concat_axis=0,
-            tiled=True,
+        lane_wait(
+            jnp.where((asked_ids >= 0)[:, :, None, None], found, jnp.zeros((), jnp.bfloat16))
         ),
         asked_ids,
     )

time: 829 us -> 823 us (level)
  waiting for transfers between devices: 243 us -> 186 us
  local copies, waits for them, and re-layouts: 62 us -> 83.2 us
  other arithmetic: 145 us -> 162 us
    all_to_all x1 -> x0, waiting for transfers between devices: 87.1 us -> none  [body(): lax.all_to_all(jnp.where((asked_ids >= 0)[:, :, None, None], found, jnp.z...]
    ppermute x0 -> x7, waiting for transfers between devices: none -> 82.6 us  [lane_wait(): ppermute(mat_out, axis_name='narrow', perm=[(tick, (tick + at) % odd) for...]
    all_gather x1, waiting for transfers between devices: 31.1 us -> 0.01 us  [body(): fragment = lax.all_gather(centroids_src, 'narrow', axis=0, tiled=True)]
    all_gather x1, waiting for transfers between devices: 20.9 us -> 0.01 us  [body(): col_panel = lax.all_gather(centroids_tgt, 'wide', axis=1, tiled=True)]
    concatenate x0 -> x2, other arithmetic: none -> 18.3 us  [the longest x1 9.14 us: lane_wait(): newest = jnp.roll(field, -vec_out * big, 0)]
    unnamed x25 -> x30, local copies, waits for them, and re-layouts: 0.91 us -> 13.8 us
  transfers between devices with their start and end apart: 13 -> 19, of which waited for: 11 -> 13; matrix products, arithmetic and copies ran while one was open for 8% -> 14% of each run, Pallas kernels for 0% -> 0%
where the time goes in v1:
time: 823 us; the launch traced here: 815 us
  blocking collectives  294 us (36%)
  waiting for transfers between devices  186 us (23%)
  other arithmetic  162 us (20%)
  local copies, waits for them, and re-layouts  83.2 us (10%)
  starting transfers between devices  43.7 us (5%)
  matrix products  30.1 us (4%)
  between operations  14.9 us (2%)
    all_to_all x1, waiting for transfers between devices, body(): lax.all_to_all(row_slots, 'narrow', split_axis=0, concat_axis=0, tiled=True)  82.9 us
    ppermute x7, waiting for transfers between devices, lane_wait(): ppermute(mat_out, axis_name='narrow', perm=[(tick, (tick + at) % odd) for...  82.6 us
    pmax x6, blocking collectives, lateral_lse_offset(): best_rating = lax.pmax(jnp.max(rating_grid_form, axis=1), 'narrow')  75.5 us
    psum x6, blocking collectives, lateral_lse_offset(): lax.psum(jnp.sum(jnp.exp(rating_grid_form - best_rating[:, None]), axis=1...  72.9 us
    pmax x6, blocking collectives, vertical_lse_offset(): best_rating = lax.pmax(jnp.max(rating_grid_form, axis=0), 'wide')  63.9 us
    psum x6, blocking collectives, vertical_lse_offset(): lax.psum(jnp.sum(jnp.exp(rating_grid_form - best_rating[None, :]), axis=0...  50.3 us
    reduce_sum x6, other arithmetic, lateral_lse_offset(): jnp.sum(jnp.exp(rating_grid_form - best_rating[:, None]), axis=1)  26.6 us
    reduce_sum x6, other arithmetic, vertical_lse_offset(): jnp.sum(jnp.exp(rating_grid_form - best_rating[None, :]), axis=0)  26.2 us
  transfers between devices with their start and end apart: 19, of which 13 were waited for; matrix products, arithmetic and copies ran while one was open for 14% of the time, Pallas kernels for 0%

profile of v1, /device:TPU:0, one launch (start us, length us, event | category | flops | bytes accessed | tf_op | source)
XLA Modules:
  0.0 814.8 jit_solution(4253261963258389333)
XLA Ops:
  10.4 5.2 all-to-all-start
  20.5 5.8 gather_fusion.1
  26.3 7.4 select_select_fusion
  33.7 9.1 %fusion.3 = bf16[8,5,128,768]{3,2,1,0:T(8,128)(2,1)} fusion(s32[]{:T(128)S(6)} %select_n.233, bf16[8,5,128,768]{3,2,1,0:T(8,128)(2,1)} %select_select_fusion), kind=kLoop, calls=%fused_computation.36 | loop fusion | flops 3932160 | bytes 15728644 | tf_op jit(solution)/shard_map/jit(_roll_dynamic)/concatenate | solution.py:56
  42.8 6.1 fusion.56
  55.1 20.9 %collective-permute-done = bf16[1,5,128,768]{3,2,1,0:T(8,128)(2,1)S(1)} collective-permute-done((bf16[1,5,128,768]{3,2,1,0:T(8,128)(2,1)}, bf16[1,5,128,768]{3,2,1,0:T(8,128)(2,1)S(1)}, u32[]{:S(2)}, u32[]{:S(2)}) %collective-permute-start) | collective-permute-done | bytes 983072 | tf_op jit(solution)/shard_map/ppermute | solution.py:61
  76.8 21.5 %collective-permute-done.1 = bf16[1,5,128,768]{3,2,1,0:T(8,128)(2,1)} collective-permute-done((bf16[1,5,128,768]{3,2,1,0:T(8,128)(2,1)}, bf16[1,5,128,768]{3,2,1,0:T(8,128)(2,1)}, u32[]{:S(2)}, u32[]{:S(2)}) %collective-permute-start.1) | collective-permute-done | bytes 983072 | tf_op jit(solution)/shard_map/ppermute | solution.py:61
  106.7 19.8 %collective-permute-done.4 = bf16[1,5,128,768]{3,2,1,0:T(8,128)(2,1)} collective-permute-done((bf16[1,5,128,768]{3,2,1,0:T(8,128)(2,1)}, bf16[1,5,128,768]{3,2,1,0:T(8,128)(2,1)}, u32[]{:S(2)}, u32[]{:S(2)}) %collective-permute-start.4) | collective-permute-done | bytes 983072 | tf_op jit(solution)/shard_map/ppermute | solution.py:61
  128.8 20.3 %collective-permute-done.5 = bf16[1,5,128,768]{3,2,1,0:T(8,128)(2,1)S(1)} collective-permute-done((bf16[1,5,128,768]{3,2,1,0:T(8,128)(2,1)}, bf16[1,5,128,768]{3,2,1,0:T(8,128)(2,1)S(1)}, u32[]{:S(2)}, u32[]{:S(2)}) %collective-permute-start.5) | collective-permute-done | bytes 983072 | tf_op jit(solution)/shard_map/ppermute | solution.py:61
  153.4 9.1 %fusion.2 = bf16[8,5,128,768]{3,2,1,0:T(8,128)(2,1)} fusion(s32[]{:T(128)S(6)} %select_n.235, bf16[8,5,128,768]{3,2,1,0:T(8,128)(2,1)} %slice_dynamic-update-slice_fusion), kind=kLoop, calls=%fused_computation.35 | loop fusion | flops 3932160 | bytes 15728644 | tf_op jit(solution)/shard_map/jit(_roll_dynamic)/concatenate | solution.py:66
  162.5 6.8 gather_fusion.2
  174.1 5.7 subtract_multiply_fusion.2
  179.8 365.3 %while.11 = (s32[]{:T(128)}, f32[1024]{0:T(1024)S(1)}, f32[2048,1024]{1,0:T(8,128)}, f32[2048]{0:T(1024)S(1)}, f32[1024]{0:T(1024)S(1)}, /*index=5*/s32[]{:T(128)}, s32[]{:T(128)}) while((s32[]{:T(128)}, f32[1024]{0:T(1024)S(1)}, f32[2048,1024]{1,0:T(8,128)}, f32[2048]{0:T(1024)S(1)}, f32[1024]{0:T(1024)S(1)}, ...), condition=%wide.region_13.14_spmd.clone, body=%wide.region_4.13_spmd.clone.sunk | while | flops 29370372 | bytes 33722456 | solution.py:88
  184.1 15.2 %pmax.18 = f32[2048]{0:T(1024)S(1)} all-reduce(f32[2048]{0:T(1024)S(1)} %fusion.66), channel_id=1, replica_groups=mesh['wide'=4,'narrow'=8] {'narrow'}, use_global_device_ids=true, to_apply=%region_6.0 | all-reduce | flops 2048 | bytes 16384 | tf_op jit(solution)/shard_map/while/body/eval_jaxpr/pmax | solution.py:25
  199.2 4.4 exponential_reduce_fusion.10
  203.7 12.6 %psum.18 = f32[2048]{0:T(1024)S(1)} all-reduce(f32[2048]{0:T(1024)S(1)} %exponential_reduce_fusion.10), channel_id=1, replica_groups=mesh['wide'=4,'narrow'=8] {'narrow'}, use_global_device_ids=true, to_apply=%region_8.0 | all-reduce | flops 2048 | bytes 16384 | tf_op jit(solution)/shard_map/while/body/eval_jaxpr/psum | solution.py:26
  220.3 12.0 %pmax.19 = f32[1024]{0:T(1024)S(1)} all-reduce(f32[1024]{0:T(1024)S(1)} %fusion.67), channel_id=1, replica_groups=mesh['wide'=4,'narrow'=8] {'wide'}, use_global_device_ids=true, to_apply=%region_10.0 | all-reduce | flops 1024 | bytes 8192 | tf_op jit(solution)/shard_map/while/body/eval_jaxpr/pmax | solution.py:33
  232.2 4.4 exponential_reduce_fusion.11
  236.6 8.4 %psum.19 = f32[1024]{0:T(1024)S(1)} all-reduce(f32[1024]{0:T(1024)S(1)} %exponential_reduce_fusion.11), channel_id=1, replica_groups=mesh['wide'=4,'narrow'=8] {'wide'}, use_global_device_ids=true, to_apply=%region_12.12 | all-reduce | flops 1024 | bytes 8192 | tf_op jit(solution)/shard_map/while/body/eval_jaxpr/psum | solution.py:34
  249.3 12.0 %pmax.18 = f32[2048]{0:T(1024)S(1)} all-reduce(f32[2048]{0:T(1024)S(1)} %fusion.66), channel_id=1, replica_groups=mesh['wide'=4,'narrow'=8] {'narrow'}, use_global_device_ids=true, to_apply=%region_6.0 | all-reduce | flops 2048 | bytes 16384 | tf_op jit(solution)/shard_map/while/body/eval_jaxpr/pmax | solution.py:25
  261.3 4.4 exponential_reduce_fusion.10
  265.8 12.0 %psum.18 = f32[2048]{0:T(1024)S(1)} all-reduce(f32[2048]{0:T(1024)S(1)} %exponential_reduce_fusion.10), channel_id=1, replica_groups=mesh['wide'=4,'narrow'=8] {'narrow'}, use_global_device_ids=true, to_apply=%region_8.0 | all-reduce | flops 2048 | bytes 16384 | tf_op jit(solution)/shard_map/while/body/eval_jaxpr/psum | solution.py:26
  281.8 10.4 %pmax.19 = f32[1024]{0:T(1024)S(1)} all-reduce(f32[1024]{0:T(1024)S(1)} %fusion.67), channel_id=1, replica_groups=mesh['wide'=4,'narrow'=8] {'wide'}, use_global_device_ids=true, to_apply=%region_10.0 | all-reduce | flops 1024 | bytes 8192 | tf_op jit(solution)/shard_map/while/body/eval_jaxpr/pmax | solution.py:33
  292.2 4.4 exponential_reduce_fusion.11
  296.6 8.4 %psum.19 = f32[1024]{0:T(1024)S(1)} all-reduce(f32[1024]{0:T(1024)S(1)} %exponential_reduce_fusion.11), channel_id=1, replica_groups=mesh['wide'=4,'narrow'=8] {'wide'}, use_global_device_ids=true, to_apply=%region_12.12 | all-reduce | flops 1024 | bytes 8192 | tf_op jit(solution)/shard_map/while/body/eval_jaxpr/psum | solution.py:34
  309.3 12.0 %pmax.18 = f32[2048]{0:T(1024)S(1)} all-reduce(f32[2048]{0:T(1024)S(1)} %fusion.66), channel_id=1, replica_groups=mesh['wide'=4,'narrow'=8] {'narrow'}, use_global_device_ids=true, to_apply=%region_6.0 | all-reduce | flops 2048 | bytes 16384 | tf_op jit(solution)/shard_map/while/body/eval_jaxpr/pmax | solution.py:25
  321.3 4.4 exponential_reduce_fusion.10
  325.8 12.0 %psum.18 = f32[2048]{0:T(1024)S(1)} all-reduce(f32[2048]{0:T(1024)S(1)} %exponential_reduce_fusion.10), channel_id=1, replica_groups=mesh['wide'=4,'narrow'=8] {'narrow'}, use_global_device_ids=true, to_apply=%region_8.0 | all-reduce | flops 2048 | bytes 16384 | tf_op jit(solution)/shard_map/while/body/eval_jaxpr/psum | solution.py:26
  341.8 10.4 %pmax.19 = f32[1024]{0:T(1024)S(1)} all-reduce(f32[1024]{0:T(1024)S(1)} %fusion.67), channel_id=1, replica_groups=mesh['wide'=4,'narrow'=8] {'wide'}, use_global_device_ids=true, to_apply=%region_10.0 | all-reduce | flops 1024 | bytes 8192 | tf_op jit(solution)/shard_map/while/body/eval_jaxpr/pmax | solution.py:33
  352.2 4.4 exponential_reduce_fusion.11
  356.6 8.4 %psum.19 = f32[1024]{0:T(1024)S(1)} all-reduce(f32[1024]{0:T(1024)S(1)} %exponential_reduce_fusion.11), channel_id=1, replica_groups=mesh['wide'=4,'narrow'=8] {'wide'}, use_global_device_ids=true, to_apply=%region_12.12 | all-reduce | flops 1024 | bytes 8192 | tf_op jit(solution)/shard_map/while/body/eval_jaxpr/psum | solution.py:34
  369.2 12.0 %pmax.18 = f32[2048]{0:T(1024)S(1)} all-reduce(f32[2048]{0:T(1024)S(1)} %fusion.66), channel_id=1, replica_groups=mesh['wide'=4,'narrow'=8] {'narrow'}, use_global_device_ids=true, to_apply=%region_6.0 | all-reduce | flops 2048 | bytes 16384 | tf_op jit(solution)/shard_map/while/body/eval_jaxpr/pmax | solution.py:25
  381.3 4.4 exponential_reduce_fusion.10
  385.7 12.0 %psum.18 = f32[2048]{0:T(1024)S(1)} all-reduce(f32[2048]{0:T(1024)S(1)} %exponential_reduce_fusion.10), channel_id=1, replica_groups=mesh['wide'=4,'narrow'=8] {'narrow'}, use_global_device_ids=true, to_apply=%region_8.0 | all-reduce | flops 2048 | bytes 16384 | tf_op jit(solution)/shard_map/while/body/eval_jaxpr/psum | solution.py:26
  401.8 10.4 %pmax.19 = f32[1024]{0:T(1024)S(1)} all-reduce(f32[1024]{0:T(1024)S(1)} %fusion.67), channel_id=1, replica_groups=mesh['wide'=4,'narrow'=8] {'wide'}, use_global_device_ids=true, to_apply=%region_10.0 | all-reduce | flops 1024 | bytes 8192 | tf_op jit(solution)/shard_map/while/body/eval_jaxpr/pmax | solution.py:33
  412.2 4.4 exponential_reduce_fusion.11
  416.5 8.4 %psum.19 = f32[1024]{0:T(1024)S(1)} all-reduce(f32[1024]{0:T(1024)S(1)} %exponential_reduce_fusion.11), channel_id=1, replica_groups=mesh['wide'=4,'narrow'=8] {'wide'}, use_global_device_ids=true, to_apply=%region_12.12 | all-reduce | flops 1024 | bytes 8192 | tf_op jit(solution)/shard_map/while/body/eval_jaxpr/psum | solution.py:34
  429.2 12.0 %pmax.18 = f32[2048]{0:T(1024)S(1)} all-reduce(f32[2048]{0:T(1024)S(1)} %fusion.66), channel_id=1, replica_groups=mesh['wide'=4,'narrow'=8] {'narrow'}, use_global_device_ids=true, to_apply=%region_6.0 | all-reduce | flops 2048 | bytes 16384 | tf_op jit(solution)/shard_map/while/body/eval_jaxpr/pmax | solution.py:25
  441.3 4.4 exponential_reduce_fusion.10
  445.7 12.0 %psum.18 = f32[2048]{0:T(1024)S(1)} all-reduce(f32[2048]{0:T(1024)S(1)} %exponential_reduce_fusion.10), channel_id=1, replica_groups=mesh['wide'=4,'narrow'=8] {'narrow'}, use_global_device_ids=true, to_apply=%region_8.0 | all-reduce | flops 2048 | bytes 16384 | tf_op jit(solution)/shard_map/while/body/eval_jaxpr/psum | solution.py:26
  461.8 10.4 %pmax.19 = f32[1024]{0:T(1024)S(1)} all-reduce(f32[1024]{0:T(1024)S(1)} %fusion.67), channel_id=1, replica_groups=mesh['wide'=4,'narrow'=8] {'wide'}, use_global_device_ids=true, to_apply=%region_10.0 | all-reduce | flops 1024 | bytes 8192 | tf_op jit(solution)/shard_map/while/body/eval_jaxpr/pmax | solution.py:33
  472.1 4.4 exponential_reduce_fusion.11
  476.5 8.4 %psum.19 = f32[1024]{0:T(1024)S(1)} all-reduce(f32[1024]{0:T(1024)S(1)} %exponential_reduce_fusion.11), channel_id=1, replica_groups=mesh['wide'=4,'narrow'=8] {'wide'}, use_global_device_ids=true, to_apply=%region_12.12 | all-reduce | flops 1024 | bytes 8192 | tf_op jit(solution)/shard_map/while/body/eval_jaxpr/psum | solution.py:34
  489.2 12.1 %pmax.18 = f32[2048]{0:T(1024)S(1)} all-reduce(f32[2048]{0:T(1024)S(1)} %fusion.66), channel_id=1, replica_groups=mesh['wide'=4,'narrow'=8] {'narrow'}, use_global_device_ids=true, to_apply=%region_6.0 | all-reduce | flops 2048 | bytes 16384 | tf_op jit(solution)/shard_map/while/body/eval_jaxpr/pmax | solution.py:25
  501.3 4.4 exponential_reduce_fusion.10
  505.8 12.1 %psum.18 = f32[2048]{0:T(1024)S(1)} all-reduce(f32[2048]{0:T(1024)S(1)} %exponential_reduce_fusion.10), channel_id=1, replica_groups=mesh['wide'=4,'narrow'=8] {'narrow'}, use_global_device_ids=true, to_apply=%region_8.0 | all-reduce | flops 2048 | bytes 16384 | tf_op jit(solution)/shard_map/while/body/eval_jaxpr/psum | solution.py:26
  521.9 10.4 %pmax.19 = f32[1024]{0:T(1024)S(1)} all-reduce(f32[1024]{0:T(1024)S(1)} %fusion.67), channel_id=1, replica_groups=mesh['wide'=4,'narrow'=8] {'wide'}, use_global_device_ids=true, to_apply=%region_10.0 | all-reduce | flops 1024 | bytes 8192 | tf_op jit(solution)/shard_map/while/body/eval_jaxpr/pmax | solution.py:33
  536.7 8.4 %psum.19 = f32[1024]{0:T(1024)S(1)} all-reduce(f32[1024]{0:T(1024)S(1)} %exponential_reduce_fusion.11), channel_id=1, replica_groups=mesh['wide'=4,'narrow'=8] {'wide'}, use_global_device_ids=true, to_apply=%region_12.12 | all-reduce | flops 1024 | bytes 8192 | tf_op jit(solution)/shard_map/while/body/eval_jaxpr/psum | solution.py:34
  545.1 9.8 %all_gather.11 = f32[8192]{0:T(1024)S(1)} all-gather(f32[1024]{0:T(1024)S(1)} %get-tuple-element.34), channel_id=1, replica_groups=mesh['wide'=4,'narrow'=8] {'narrow'}, dimensions={0}, use_global_device_ids=true | all-gather | bytes 36864 | tf_op jit(solution)/shard_map/all_gather | solution.py:91
  554.9 6.1 gather_fusion
  565.9 4.6 multiply_reduce_fusion
  571.3 4.9 fusion.13
  591.8 4.6 all-to-all-done.3
  597.2 7.2 all_to_all.69
  621.5 4.6 all-to-all-done.6
  627.0 7.2 all_to_all.70
  653.9 4.6 all-to-all-done.9
  659.4 7.2 all_to_all.71
  674.7 4.5 convolution_convert_fusion
  683.2 20.1 %scatter_fusion = bf16[40,128,768]{2,1,0:T(8,128)(2,1)} fusion(bf16[40,128,768]{2,1,0:T(8,128)(2,1)} %broadcast_in_dim.228, s32[32]{0:T(128)S(1)} %fusion.50, bf16[32,128,768]{2,1,0:T(8,128)(2,1)} %bitcast.88), kind=kCustom, calls=%fused_computation.18 | custom fusion | bytes 18874496 | tf_op jit(solution)/shard_map/scatter | solution.py:119
  703.3 4.9 all-to-all-start.11
  708.4 5.2 fusion.9
  713.8 82.9 %all-to-all-done.11 = bf16[8,5,128,768]{3,2,1,0:T(8,128)(2,1)} async-done(((bf16[8,5,128,768]{3,2,1,0:T(8,128)(2,1)}), bf16[8,5,128,768]{3,2,1,0:T(8,128)(2,1)}, u32[]{:S(2)}, u32[]{:S(2)}) %all-to-all-start.11) | async-done | bytes 7864352 | tf_op jit(solution)/shard_map/all_to_all | solution.py:218
  796.6 9.7 %divide_convert_fusion = bf16[8,128,768]{2,0,1:T(8,128)(2,1)S(1)} fusion(f32[8,128]{0,1:T(8,128)S(1)} %fusion.43, s32[40]{0:T(128)S(1)} %reshape.452, bf16[5,8,128,768]{3,2,1,0:T(8,128)(2,1)} %bitcast.46), kind=kOutput, calls=%fused_computation.48 | convolution fusion | flops 64487744 | bytes 9441440 | tf_op jit(solution)/shard_map/dot_general | solution.py:224
  (198 shorter events, 162.6 us)
Async XLA Ops:
  7.2 13.4 %copy-start = (bf16[1024,768]{1,0:T(8,128)(2,1)S(1)}, bf16[1024,768]{1,0:T(8,128)(2,1)}, u32[]{:S(2)}) copy-start(bf16[1024,768]{1,0:T(8,128)(2,1)} %param.17) | copy-start | bytes 4718596
  7.2 162.2 %all-gather.5.cloned.1.call-start = ((), (), s32[]{:S(2)}) async-start(), calls=%async_computation.14 | async-start | bytes 1966080 | tf_op jit(solution)/shard_map/all_gather | solution.py:71
  10.4 9.8 %all-to-all-start = ((s32[8,1,5]{2,1,0:T(1,128)}), s32[8,1,5]{2,1,0:T(1,128)S(1)}, u32[]{:S(2)}, u32[]{:S(2)}) async-start(s32[8,1,5]{2,1,0:T(1,128)} %bitcast.2), calls=%async_computation | async-start | bytes 8192 | tf_op jit(solution)/shard_map/all_to_all | solution.py:121
  15.6 155.6 %all-gather.3.cloned.1.call-start = ((), (), s32[]{:S(2)}) async-start(), calls=%async_computation.13 | async-start | bytes 3538944 | tf_op jit(solution)/shard_map/all_gather | solution.py:73
  42.8 7.6 copy-start.10
  42.8 8.1 copy-start.5
  48.9 27.1 %collective-permute-start = (bf16[1,5,128,768]{3,2,1,0:T(8,128)(2,1)}, bf16[1,5,128,768]{3,2,1,0:T(8,128)(2,1)S(1)}, u32[]{:S(2)}, u32[]{:S(2)}) collective-permute-start(bf16[1,5,128,768]{3,2,1,0:T(8,128)(2,1)} %get-tuple-element.75), channel_id=1, source_target_pairs={{0,7},{1,0},{2,1},{3,2},{4,3},{5,4},{6,5},{7,6},{8,15},{9,8},{10,9... | collective-permute-start | bytes 2949128 | tf_op jit(solution)/shard_map/ppermute | solution.py:61
  49.3 49.1 %collective-permute-start.1 = (bf16[1,5,128,768]{3,2,1,0:T(8,128)(2,1)}, bf16[1,5,128,768]{3,2,1,0:T(8,128)(2,1)}, u32[]{:S(2)}, u32[]{:S(2)}) collective-permute-start(bf16[1,5,128,768]{3,2,1,0:T(8,128)(2,1)} %get-tuple-element.74), channel_id=1, source_target_pairs={{0,6},{1,7},{2,0},{3,1},{4,2},{5,3},{6,4},{7,5},{8,14},{9,15},{10,... | collective-permute-start | bytes 2949128 | tf_op jit(solution)/shard_map/ppermute | solution.py:61
  50.5 51.8 %collective-permute-start.2 = (bf16[1,5,128,768]{3,2,1,0:T(8,128)(2,1)}, bf16[1,5,128,768]{3,2,1,0:T(8,128)(2,1)}, u32[]{:S(2)}, u32[]{:S(2)}) collective-permute-start(bf16[1,5,128,768]{3,2,1,0:T(8,128)(2,1)} %get-tuple-element.73), channel_id=1, source_target_pairs={{0,5},{1,6},{2,7},{3,0},{4,1},{5,2},{6,3},{7,4},{8,13},{9,14},{10,... | collective-permute-start | bytes 2949128 | tf_op jit(solution)/shard_map/ppermute | solution.py:61
  51.3 53.2 %collective-permute-start.3 = (bf16[1,5,128,768]{3,2,1,0:T(8,128)(2,1)}, bf16[1,5,128,768]{3,2,1,0:T(8,128)(2,1)}, u32[]{:S(2)}, u32[]{:S(2)}) collective-permute-start(bf16[1,5,128,768]{3,2,1,0:T(8,128)(2,1)} %get-tuple-element.72), channel_id=1, source_target_pairs={{0,4},{1,5},{2,6},{3,7},{4,0},{5,1},{6,2},{7,3},{8,12},{9,13},{10,... | collective-permute-start | bytes 2949128 | tf_op jit(solution)/shard_map/ppermute | solution.py:61
  52.4 74.2 %collective-permute-start.4 = (bf16[1,5,128,768]{3,2,1,0:T(8,128)(2,1)}, bf16[1,5,128,768]{3,2,1,0:T(8,128)(2,1)}, u32[]{:S(2)}, u32[]{:S(2)}) collective-permute-start(bf16[1,5,128,768]{3,2,1,0:T(8,128)(2,1)} %get-tuple-element.71), channel_id=1, source_target_pairs={{0,3},{1,4},{2,5},{3,6},{4,7},{5,0},{6,1},{7,2},{8,11},{9,12},{10,... | collective-permute-start | bytes 2949128 | tf_op jit(solution)/shard_map/ppermute | solution.py:61
  76.0 73.1 %collective-permute-start.5 = (bf16[1,5,128,768]{3,2,1,0:T(8,128)(2,1)}, bf16[1,5,128,768]{3,2,1,0:T(8,128)(2,1)S(1)}, u32[]{:S(2)}, u32[]{:S(2)}) collective-permute-start(bf16[1,5,128,768]{3,2,1,0:T(8,128)(2,1)} %get-tuple-element.70), channel_id=1, source_target_pairs={{0,2},{1,3},{2,4},{3,5},{4,6},{5,7},{6,0},{7,1},{8,10},{9,11},{10,... | collective-permute-start | bytes 2949128 | tf_op jit(solution)/shard_map/ppermute | solution.py:61
  98.4 51.8 %collective-permute-start.6 = (bf16[1,5,128,768]{3,2,1,0:T(8,128)(2,1)}, bf16[1,5,128,768]{3,2,1,0:T(8,128)(2,1)S(1)}, u32[]{:S(2)}, u32[]{:S(2)}) collective-permute-start(bf16[1,5,128,768]{3,2,1,0:T(8,128)(2,1)} %get-tuple-element.69), channel_id=1, source_target_pairs={{0,1},{1,2},{2,3},{3,4},{4,5},{5,6},{6,7},{7,0},{8,9},{9,10},{10,1... | collective-permute-start | bytes 2949128 | tf_op jit(solution)/shard_map/ppermute | solution.py:61
  169.4 4.7 copy-start.7
  171.3 2.8 copy-start.6
  545.1 16.0 %copy-start.9 = (s32[1024]{0:T(1024)S(1)}, s32[1024]{0:T(1024)}, u32[]{:S(2)}) copy-start(s32[1024]{0:T(1024)} %param.19) | copy-start | bytes 12292
  562.4 8.3 %all-to-all-start.1 = ((f32[8,5,128]{2,1,0:T(8,128)}), f32[8,5,128]{2,1,0:T(8,128)S(1)}, u32[]{:S(2)}, u32[]{:S(2)}) async-start(f32[8,5,128]{2,1,0:T(8,128)} %reshape.453), calls=%async_computation.1 | async-start | bytes 65536 | tf_op jit(solution)/shard_map/all_to_all | solution.py:150
  576.2 1.4 copy-start.2
  579.5 8.8 %all-to-all-start.2 = ((f32[8,5,128]{2,1,0:T(8,128)}), f32[8,5,128]{2,1,0:T(8,128)S(1)}, u32[]{:S(2)}, u32[]{:S(2)}) async-start(f32[8,5,128]{2,1,0:T(8,128)} %reshape.459), calls=%async_computation.2 | async-start | bytes 65536 | tf_op jit(solution)/shard_map/all_to_all | solution.py:174
  588.3 8.1 all-to-all-start.3
  605.0 2.2 copy-start.3
  609.9 8.1 all-to-all-start.5
  618.1 8.1 all-to-all-start.6
  638.8 31.0 %copy-start.8 = (f32[8,128]{1,0:T(8,128)}, f32[8,128]{1,0:T(8,128)S(1)}, u32[]{:S(2)}) copy-start(f32[8,128]{1,0:T(8,128)S(1)} %add_multiply_fusion.1) | copy-start | bytes 12292
  642.3 8.1 all-to-all-start.8
  650.4 8.1 all-to-all-start.9
  658.7 20.4 %copy-start.4 = (f32[8,128]{1,0:T(8,128)}, f32[8,128]{1,0:T(8,128)S(1)}, u32[]{:S(2)}) copy-start(f32[8,128]{1,0:T(8,128)S(1)} %add_multiply_fusion) | copy-start | bytes 12292
  671.1 32.2 %all-to-all-start.12 = ((bf16[8,5,128]{2,1,0:T(8,128)(2,1)}), bf16[8,5,128]{2,1,0:T(8,128)(2,1)S(1)}, u32[]{:S(2)}, u32[]{:S(2)}) async-start(bf16[8,5,128]{2,1,0:T(8,128)(2,1)} %reshape.480), calls=%async_computation.12 | async-start | bytes 32768 | tf_op jit(solution)/shard_map/all_to_all | solution.py:219
  703.3 93.3 %all-to-all-start.11 = ((bf16[8,5,128,768]{3,2,1,0:T(8,128)(2,1)}), bf16[8,5,128,768]{3,2,1,0:T(8,128)(2,1)}, u32[]{:S(2)}, u32[]{:S(2)}) async-start(bf16[8,5,128,768]{3,2,1,0:T(8,128)(2,1)} %bitcast.83), calls=%async_computation.11 | async-start | bytes 15728640 | tf_op jit(solution)/shard_map/all_to_all | solution.py:218
  796.6 11.2 %copy-start.1 = (bf16[1024,768]{1,0:T(8,128)(2,1)S(1)}, bf16[1024,768]{1,0:T(8,128)(2,1)}, u32[]{:S(2)}) copy-start(bf16[1024,768]{1,0:T(8,128)(2,1)} %param.17) | copy-start | bytes 4718596
Sparse Core Ops, SparseCore 0:
  9.6 39.7 all-gather.4
  51.3 100.8 all-gather.2
